TPU v7x, 32 devices: a whole 2x2x4 slice. The times are simulated.
32 devices in a mesh: parts: 2 (over x), pts: 16 (over z, y, core).
Axes of the slice: x: 2, y: 2, z: 4, core: 2. Of those that a mesh axis runs over, the one named last changes fastest.
Arguments:
- grid_weights: float32 [256, 128, 128], P(('parts', 'pts')), parts along dimension 0, may hold values from -6 to 6
- direction: float32 [256, 128, 128], P(('parts', 'pts')), parts along dimension 0, may hold values from -6 to 6
- kern_x: float32 [128, 128], replicated
- kern_y: float32 [128, 128], replicated
- kern_z: float32 [128, 128], replicated
- interp: bfloat16 [4096, 128, 256], P(('parts', 'pts')), parts along dimension 0, may hold values from -4 to 4
- block_corner: int32 [3, 4096], P(None, ('parts', 'pts')), parts along dimension 1, may hold values from 0 to 120, as said below
- block_offsets: int32 [4096, 256], P(('parts', 'pts')), parts along dimension 0, may hold values from 0 to 2047, as said below
- labels: int32 [4096, 128], P(('parts', 'pts')), parts along dimension 0, may hold values 0 or 1
- trial_steps: float32 [5], replicated, may hold values from 0.05 to 2
- accept: int32 [1], replicated, may hold values from 0 to 4
Outputs:
- new_weights: float32 [256, 128, 128], P(('parts', 'pts')), parts along dimension 0
- grid_gradient: float32 [256, 128, 128], P(('parts', 'pts')), parts along dimension 0
- curvature: float32 [4096, 128], P(('parts', 'pts')), parts along dimension 0
- trial_objective: float32 [10], P('parts'), parts along dimension 0
- trial_slope: float32 [10], P('parts'), parts along dimension 0
There are 2 independent parts, one for each index of `parts`. A program takes and returns all parts, laid end to end along the dimension named above; an argument that names none is the same for every part. Nothing has to cross between parts.
Inputs may be any that keep to these rules, and one draw needn't show every extreme that they name: `block_corner`: row 0 lies in 0 to 112, row 1 in 0 to 112, row 2 in 0 to 120. `block_offsets`: the 256 offsets of one block are distinct.
All inputs are finite; a program needn't handle non-finite values. No bound on the sum of `labels` on one device may be relied on, other than what follows from the above.
Results may differ from a plain program's by a relative error of at most 0.0075.
The roundings to bfloat16 on the way count: a program that leaves them out, or rounds other values in their place, can miss the bound.
Values may be sent and summed in bfloat16 or wider, within the bound.
A program may use at most 128 MiB of HBM per device.

v0:
```python
import jax
import jax.numpy as jnp
from jax import lax
from jax.sharding import PartitionSpec as P

BOXY = 16
BOXZ = 8
NTRIAL = 5


HIGHEST = lax.Precision.HIGHEST


def plane_mix(fields, kern_y, kern_z):
    inner_mix = jnp.einsum("...bc,zc->...bz", fields, kern_z, precision=HIGHEST)
    return jnp.einsum("...xbz,yb->...xyz", inner_mix, kern_y, precision=HIGHEST).astype(
        jnp.bfloat16
    )


def depth_mix(partial_value, kern_x):
    return jnp.einsum(
        "xa,...ayz->...xyz", kern_x, partial_value.astype(jnp.float32), precision=HIGHEST
    )


def cell_parts_of(block_corner, block_offsets, size_y):
    plane_off = block_offsets // (BOXY * BOXZ)
    row_off = block_offsets // BOXZ % BOXY
    depth_off = block_offsets % BOXZ
    cell_x = block_corner[0][:, None] + plane_off
    cell_y = block_corner[1][:, None] + row_off
    cell_z = block_corner[2][:, None] + depth_off
    return (cell_x * size_y + cell_y, cell_z)


def pick_cells(grid_rows, row_ids, depth_ids):
    depth_size = grid_rows.shape[-1]
    taken = jnp.take(grid_rows, row_ids, axis=1)
    depth_line = lax.broadcasted_iota(jnp.int32, (1, 1, depth_size), 2)
    wanted = depth_ids[:, :, None] == depth_line
    kept = jnp.where(wanted[None], taken, jnp.zeros((), taken.dtype))
    return jnp.sum(kept.astype(jnp.float32), axis=-1).astype(jnp.bfloat16)


def slab_add(row_ids, depth_ids, flat_terms, row_count, size_y, size_z):
    inside = (row_ids >= 0) & (row_ids < row_count * size_y)
    target_row = jnp.where(inside, row_ids, row_count * size_y)
    depth_line = lax.broadcasted_iota(jnp.int32, (1, size_z), 1)
    placed = jnp.where(depth_ids[:, None] == depth_line, flat_terms[:, None], 0.0)
    summed = (
        jnp.zeros((row_count * size_y, size_z), jnp.float32).at[target_row].add(placed, mode="drop")
    )
    return summed.reshape(row_count, size_y, size_z)


def kron_apply(fields, kern_x, kern_y, kern_z):
    partial_value = plane_mix(fields, kern_y, kern_z)
    slab_rows = fields.shape[1]
    gathered = lax.all_gather(partial_value, "pts", axis=1, tiled=True)
    mixed_grid = depth_mix(gathered, kern_x)
    slab_part = lax.dynamic_slice_in_dim(
        mixed_grid, lax.axis_index("pts") * slab_rows, slab_rows, 1
    )
    return (slab_part, mixed_grid.astype(jnp.bfloat16))


def body(
    grid_weights,
    direction,
    kern_x,
    kern_y,
    kern_z,
    interp,
    block_corner,
    block_offsets,
    labels,
    trial_steps,
    accept,
):
    slab_rows, size_y, size_z = grid_weights.shape
    devices = lax.axis_size("pts")
    points = interp.shape[0] * interp.shape[1] * devices
    row_ids, depth_ids = cell_parts_of(block_corner, block_offsets, size_y)
    slab_pair, whole_pair = kron_apply(jnp.stack([grid_weights, direction]), kern_x, kern_y, kern_z)
    quad_local = jnp.stack(
        [
            jnp.sum(grid_weights * slab_pair[0]),
            jnp.sum(direction * slab_pair[0]),
            jnp.sum(direction * slab_pair[1]),
        ]
    )
    quadratics = lax.psum(quad_local, "pts")
    values = pick_cells(whole_pair.reshape(2, -1, size_z), row_ids, depth_ids)
    latent_pair = jnp.einsum("bpc,fbc->fbp", interp, values, preferred_element_type=jnp.float32)
    latent = latent_pair[0]
    slope_pt = latent_pair[1]
    target = labels.astype(jnp.float32)
    signed = 2.0 * target - 1.0
    trial_latent = latent[None] + trial_steps[:, None, None] * slope_pt[None]
    loglik_local = jnp.sum(jax.nn.log_sigmoid(signed[None] * trial_latent), axis=(1, 2))
    descent_local = jnp.sum(
        (target[None] - jax.nn.sigmoid(trial_latent)) * slope_pt[None], axis=(1, 2)
    )
    loglik, descent = lax.psum((loglik_local, descent_local), "pts")
    prior = 0.5 * (
        quadratics[0]
        + 2.0 * trial_steps * quadratics[1]
        + trial_steps * trial_steps * quadratics[2]
    )
    trial_objective = (loglik - prior) / points
    trial_slope = (descent - quadratics[1] - trial_steps * quadratics[2]) / points
    chosen = jnp.sum(jnp.where(jnp.arange(NTRIAL) == accept[0], trial_steps, 0.0))
    probability = jax.nn.sigmoid(latent + chosen * slope_pt)
    residual = (target - probability).astype(jnp.bfloat16)
    column_term = jnp.einsum("bpc,bp->bc", interp, residual, preferred_element_type=jnp.float32)
    flat_rows = row_ids.reshape(-1)
    flat_depths = depth_ids.reshape(-1)
    flat_terms = column_term.reshape(-1)
    spread = lax.psum_scatter(
        slab_add(
            flat_rows, flat_depths, flat_terms, slab_rows * lax.axis_size("pts"), size_y, size_z
        ),
        "pts",
        scatter_dimension=0,
        tiled=True,
    )
    new_weights = grid_weights + chosen * direction
    grid_gradient = spread - new_weights
    unused_slab, bend_whole = kron_apply(grid_gradient[None], kern_x, kern_y, kern_z)
    bend_values = pick_cells(bend_whole.reshape(1, -1, size_z), row_ids, depth_ids)
    bend_pt = jnp.einsum("bpc,fbc->fbp", interp, bend_values, preferred_element_type=jnp.float32)[0]
    curvature = probability * (1.0 - probability) * bend_pt
    return (new_weights, grid_gradient, curvature, trial_objective, trial_slope)


def solution(mesh):
    return jax.shard_map(
        body,
        mesh=mesh,
        in_specs=(
            P(("parts", "pts"), None, None),
            P(("parts", "pts"), None, None),
            P(),
            P(),
            P(),
            P(("parts", "pts"), None, None),
            P(None, ("parts", "pts")),
            P(("parts", "pts"), None),
            P(("parts", "pts"), None),
            P(),
            P(),
        ),
        out_specs=(
            P(("parts", "pts"), None, None),
            P(("parts", "pts"), None, None),
            P(("parts", "pts"), None),
            P("parts"),
            P("parts"),
        ),
        check_vma=False,
    )
```

profile of v0, /device:TPU:0, one launch (start us, length us, event | category | flops | bytes accessed | tf_op | source)
XLA Modules:
  0.0 985.3 jit_solution(7694529611736947677)
XLA Ops:
  7.2 2.3 fusion.21
  9.5 2.6 fusion.16
  13.6 1.0 fusion.66
  14.7 1.2 compare_and_fusion
  16.1 1.3 fusion.53
  18.4 6.6 iota_compare_fusion.1
  25.3 64.1 %all-gather.3.cloned.1.call-done = bf16[2,128,128,128]{2,3,1,0:T(8,128)(2,1)} async-done(((bf16[2,8,128,128]{2,3,1,0:T(8,128)(2,1)}), bf16[2,128,128,128]{2,3,1,0:T(8,128)(2,1)}) %all-gather.3.cloned.1.call-update) | async-done | bytes 8388624 | tf_op jit(solution)/shard_map/all_gather | solution.py:60
  89.4 12.4 %copy.43 = bf16[2,128,128,128]{3,1,2,0:T(8,128)(2,1)} copy(bf16[2,128,128,128]{2,3,1,0:T(8,128)(2,1)} %all-gather.3.cloned.1.call-done) | data formatting | bytes 16777216 | tf_op jit(solution)/shard_map/all_gather | solution.py:60
  101.8 9.7 fusion.42
  111.6 5.7 copy-done.1
  117.3 4.1 convert_bitcast_fusion
  121.4 12.0 %copy.44 = bf16[2,128,128,128]{3,2,1,0:T(8,128)(2,1)} copy(bf16[2,128,128,128]{3,1,2,0:T(8,128)(2,1)} %convert_bitcast_fusion) | data formatting | bytes 16777216 | tf_op jit(solution)/shard_map/convert_element_type | solution.py:65
  133.4 16.4 %copy.45 = bf16[2,16384,128]{2,0,1:T(2,128)(2,1)} copy(bf16[2,16384,128]{2,1,0:T(8,128)(2,1)} %bitcast.121) | data formatting | bytes 16777216 | tf_op jit(solution)/shard_map/reshape | solution.py:94
  149.8 214.5 %gather_fusion = bf16[32768,2,128]{2,1,0:T(2,128)(2,1)} fusion(bf16[2,16384,128]{2,0,1:T(2,128)(2,1)} %copy.45, s32[32768]{0:T(1024)S(1)} %broadcast_clamp_fusion), kind=kCustom, calls=%fused_computation | custom fusion | bytes 33685504 | tf_op jit(solution)/shard_map/jit(_take)/gather | solution.py:39
  364.3 97.9 %fusion.2 = bf16[128,256,2]{2,1,0:T(8,128)(2,1)} fusion(bf16[128,256,2,128]{3,2,1,0:T(2,128)(2,1)} %bitcast.118, pred[128,256]{1,0:T(8,128)(4,1)S(1)} %get-tuple-element.15, pred[128,256,128]{2,1,0:T(8,128)(4,1)} %iota_compare_fusion.1), kind=kLoop, calls=%fused_computation.10 | loop fusion | flops 25100288 | bytes 21135360 | tf_op jit(solution)/shard_map/reduce_sum | solution.py:43
  462.2 8.1 fusion.18
  471.1 4.6 fusion.50
  475.8 198.6 %scatter_custom_fusion = f32[16384,128]{1,0:T(8,128)} fusion(s32[32768]{0:T(1024)S(1)} %bitcast.138, f32[]{:T(128)} %constant.89.clone.1, f32[32768]{0:T(1024)S(1)} %bitcast.133, s32[32768]{0:T(1024)S(1)} %bitcast.132), kind=kCustom, calls=%fused_computation.6 | custom fusion | flops 12582912 | bytes 8651776 | tf_op jit(solution)/shard_map/scatter-add | solution.py:52
  674.5 102.2 %reduce-scatter.2.cloned.1.call-done = f32[8,128,128]{2,1,0:T(8,128)} async-done(((f32[128,128,128]{2,1,0:T(8,128)}), f32[8,128,128]{2,1,0:T(8,128)}) %reduce-scatter.2.cloned.1.call-update) | async-done | bytes 524304 | tf_op jit(solution)/shard_map/reduce_scatter | solution.py:120
  776.7 2.5 fusion.55
  781.9 1.3 dynamic-slice_bitcast_fusion
  783.1 1.3 multiply_reduce_fusion
  784.4 2.0 pad_maximum_fusion
  786.4 33.4 %all-reduce = (f32[5]{0:T(128)S(1)}, f32[3]{0:T(128)S(1)}, f32[5]{0:T(128)S(1)}) all-reduce(f32[5]{0:T(128)S(1)} %neg.22, f32[3]{0:T(128)S(1)} %pad_maximum_fusion, f32[5]{0:T(128)S(1)} %get-tuple-element.8), channel_id=1, replica_groups=mesh['parts'=2,'pts'=16] {'pts'}, use_global_device_ids=true, to_apply=%region_6.7 | all-reduce | flops 13 | bytes 104 | tf_op jit(solution)/shard_map/psum | solution.py:105
  821.0 2.4 subtract_multiply_fusion.1
  823.5 8.2 all-gather.5.cloned.1.call-done
  831.6 7.2 convert_bitcast_fusion.1
  838.8 4.7 copy.51
  843.5 112.1 %gather_fusion.1 = bf16[32768,128]{1,0:T(8,128)(2,1)} fusion(bf16[16384,128]{1,0:T(8,128)(2,1)} %bitcast.117, s32[32768]{0:T(1024)S(1)} %broadcast_clamp_fusion), kind=kCustom, calls=%fused_computation.1 | custom fusion | bytes 16908288 | tf_op jit(solution)/shard_map/jit(_take)/gather | solution.py:39
  955.6 15.7 %fusion.4 = bf16[128,256]{1,0:T(8,128)(2,1)S(1)} fusion(bf16[1,128,256,128]{3,2,1,0:T(8,128)(2,1)} %bitcast.119, s32[128,256]{1,0:T(8,128)S(1)} %fusion.35, pred[128,256]{1,0:T(8,128)(4,1)S(1)} %get-tuple-element.15), kind=kLoop, calls=%fused_computation.12 | loop fusion | flops 16744448 | bytes 8617984 | tf_op jit(solution)/shard_map/reduce_sum | solution.py:43
  971.4 5.6 fusion.36
  977.0 1.3 fusion.41
  (42 shorter events, 6.6 us)
Async XLA Ops:
  7.2 94.7 %copy-start = (f32[128,128]{1,0:T(8,128)S(1)}, f32[128,128]{1,0:T(8,128)}, u32[]{:S(2)}) copy-start(f32[128,128]{1,0:T(8,128)} %param.13) | copy-start | bytes 196612
  7.2 82.2 %all-gather.3.cloned.1.call-start = ((), (), s32[]{:S(2)}) async-start(), calls=%async_computation.1 | async-start | bytes 8912896 | tf_op jit(solution)/shard_map/all_gather | solution.py:60
  12.1 764.6 %reduce-scatter.2.cloned.1.call-start = ((), (), s32[]{:S(2)}) async-start(), calls=%async_computation.2 | async-start | bytes 8912896 | tf_op jit(solution)/shard_map/reduce_scatter | solution.py:120
  111.6 5.7 copy-start.1
  462.2 8.2 copy-start.6
  475.8 301.0 %copy-start.2 = (f32[8,128,128]{2,1,0:T(8,128)S(1)}, f32[8,128,128]{2,1,0:T(8,128)}, u32[]{:S(2)}) copy-start(f32[8,128,128]{2,1,0:T(8,128)} %param.12) | copy-start | bytes 1572868
  475.8 300.9 %copy-start.3 = (f32[8,128,128]{2,1,0:T(8,128)S(1)}, f32[8,128,128]{2,1,0:T(8,128)}, u32[]{:S(2)}) copy-start(f32[8,128,128]{2,1,0:T(8,128)} %param.11) | copy-start | bytes 1572868
  475.8 303.5 %copy-start.5 = (f32[128,128]{1,0:T(8,128)S(1)}, f32[128,128]{1,0:T(8,128)}, u32[]{:S(2)}) copy-start(f32[128,128]{1,0:T(8,128)} %param.15) | copy-start | bytes 196612
  475.8 304.1 %copy-start.7 = (f32[128,128]{1,0:T(8,128)S(1)}, f32[128,128]{1,0:T(8,128)}, u32[]{:S(2)}) copy-start(f32[128,128]{1,0:T(8,128)} %param.14) | copy-start | bytes 196612
  674.4 106.9 %copy-start.8 = (f32[5]{0:T(128)S(1)}, f32[5]{0:T(128)}, u32[]{:S(2)}) copy-start(f32[5]{0:T(128)} %param.20) | copy-start | bytes 64
  674.5 157.1 %all-gather.5.cloned.1.call-start = ((), (), s32[]{:S(2)}) async-start(), calls=%async_computation.3 | async-start | bytes 4456448 | tf_op jit(solution)/shard_map/all_gather | solution.py:60
  779.3 64.3 %copy-start.4 = (f32[8,128,128]{2,1,0:T(8,128)}, f32[8,128,128]{2,1,0:T(8,128)S(1)}, u32[]{:S(2)}) copy-start(f32[8,128,128]{2,1,0:T(8,128)S(1)} %get-tuple-element.13) | copy-start | bytes 1572868
Sparse Core Ops, SparseCore 0:
  12.3 77.0 all-gather.2
  674.6 102.0 reduce-scatter.1
  781.5 50.1 all-gather.4
where the time goes:
time: 989 us; the launch traced here: 985 us
  local copies, waits for them, and re-layouts  382 us (39%)
  other arithmetic  338 us (34%)
  waiting for transfers between devices  174 us (18%)
  matrix products  41.3 us (4%)
  blocking collectives  33.4 us (3%)
  between operations  15.6 us (2%)
    gather x2, local copies, waits for them, and re-layouts, pick_cells(): taken = jnp.take(grid_rows, row_ids, axis=1)  327 us
    scatter-add x1, other arithmetic, slab_add(): jnp.zeros((row_count * size_y, size_z), jnp.float32).at[target_row]  199 us
    reduce_sum x2, other arithmetic, pick_cells(): return jnp.sum(kept.astype(jnp.float32), axis=-1).astype(jnp.bfloat16)  114 us
    reduce_scatter x1, waiting for transfers between devices, body(): lax.psum_scatter(slab_add(flat_rows, flat_depths, flat_terms, slab_rows *...  102 us
    all_gather x2, waiting for transfers between devices, kron_apply(): gathered = lax.all_gather(partial_value, 'pts', axis=1, tiled=True)  72.2 us
    psum x1, blocking collectives, body(): loglik, descent = lax.psum((loglik_local, descent_local), 'pts')  33.4 us
  transfers between devices with their start and end apart: 3, of which 3 were waited for; matrix products, arithmetic and copies ran while one was open for 2% of the time, Pallas kernels for 0%

commit v1 on v0

v1 whole, which is shorter than its diff:
```python
import functools

import jax
import jax.numpy as jnp
from jax import lax
from jax.experimental import pallas as pl
from jax.experimental.pallas import tpu as pltpu
from jax.sharding import PartitionSpec as P

BOXX = 16
BOXY = 16
BOXZ = 8
NTRIAL = 5
PACK = 16
VMEM_BYTES = 60 * 1024 * 1024

HIGHEST = lax.Precision.HIGHEST
F32 = jnp.float32
BF16 = jnp.bfloat16
NT = (((1,), (1,)), ((), ()))


def high_part(value):
    return lax.reduce_precision(value, 8, 7)


def plane_mix(fields_zc, kern_y, kern_z):
    inner = jnp.einsum("zc,fabc->zfab", kern_z, fields_zc, precision=HIGHEST)
    return jnp.einsum("zfab,yb->zfay", inner, kern_y, precision=HIGHEST).astype(BF16)


def widen_kern(kern_x, devices, slab, group):
    size_x = kern_x.shape[0]
    parts = kern_x.reshape(1, size_x, devices, 1, slab)
    same = jnp.eye(group, dtype=F32).reshape(group, 1, 1, group, 1)
    wide = (parts * same).reshape(group * size_x, devices * group * slab)
    high = high_part(wide)
    return high.astype(BF16), (wide - high).astype(BF16)


def mix_depth(planes_ref, kh_ref, kl_ref, image, group, size_x):
    devices, units, pack, lanes = planes_ref.shape

    def one(step, carry):
        pair = [
            planes_ref[:, step * 2 + t].reshape(devices * pack, lanes) for t in range(2)
        ]
        rhs = jnp.concatenate(pair, axis=1)
        mixed = jnp.dot(kh_ref[...], rhs, preferred_element_type=F32)
        mixed = mixed + jnp.dot(kl_ref[...], rhs, preferred_element_type=F32)
        for t in range(2):
            for g in range(group):
                image[(step * 2 + t) * group + g] = mixed[
                    g * size_x : (g + 1) * size_x, t * lanes : (t + 1) * lanes
                ]
        return carry

    lax.fori_loop(0, units // 2, one, 0)


def pick_values(image, corner_ref, y_ref, row_ref, block, local, fields):
    size_y = image.shape[-1]
    cols = y_ref.shape[-1]
    box_rows = BOXZ * BOXX
    at_z = corner_ref[2, block]
    at_x = corner_ref[0, block]
    box = image[pl.ds(at_z * fields, BOXZ * fields), pl.ds(at_x, BOXX), :]
    box = box.reshape(fields * box_rows, size_y).astype(BF16)
    y_line = lax.broadcasted_iota(jnp.int32, (size_y, cols), 0)
    pick_y = jnp.where(y_line == y_ref[pl.ds(local, 1), :], 1.0, 0.0).astype(BF16)
    lines = jnp.dot(box, pick_y, preferred_element_type=F32)
    lines = lines.reshape(BOXZ, fields, BOXX, cols)
    row_line = lax.broadcasted_iota(jnp.int32, (box_rows, cols), 0)
    kept = row_line == row_ref[pl.ds(local, 1), :]
    top = lax.broadcasted_iota(jnp.int32, (8, cols), 0)
    stacked = jnp.zeros((8, cols), F32)
    for f in range(fields):
        line = jnp.where(kept, lines[:, f].reshape(box_rows, cols), 0.0)
        value = jnp.sum(line, axis=0, keepdims=True)
        stacked = jnp.where(top == f, value, stacked)
    return stacked.astype(BF16)


def forward_kernel(
    group,
    unroll,
    corner_ref,
    slab_ref,
    chosen_ref,
    planes_ref,
    kh_ref,
    kl_ref,
    y_ref,
    row_ref,
    labels_ref,
    interp_ref,
    latent_ref,
    prob_ref,
    col_ref,
    own_ref,
    image,
    res_ref,
):
    step = pl.program_id(0)
    count = interp_ref.shape[0]
    size_x = image.shape[1]

    @pl.when(step == 0)
    def _():
        mix_depth(planes_ref, kh_ref, kl_ref, image, group, size_x)
        slab = own_ref.shape[1]
        at = pl.multiple_of(slab_ref[0] * slab, slab)
        own_ref[...] = image[:, pl.ds(at, slab), :]

    def some(part, carry):
        for k in range(unroll):
            local = part * unroll + k
            values = pick_values(
                image, corner_ref, y_ref, row_ref, step * count + local, local, 2
            )
            pair = lax.dot_general(values, interp_ref[local], NT, preferred_element_type=F32)
            latent_ref[0, pl.ds(local, 1), :] = pair[0:1]
            latent_ref[1, pl.ds(local, 1), :] = pair[1:2]
        return carry

    lax.fori_loop(0, count // unroll, some, 0)
    logits = latent_ref[0] + chosen_ref[0] * latent_ref[1]
    prob = jax.nn.sigmoid(logits)
    prob_ref[...] = prob
    res_ref[...] = (labels_ref[...].astype(F32) - prob).astype(BF16).astype(F32)

    def back(part, carry):
        for k in range(unroll):
            local = part * unroll + k
            row = jnp.broadcast_to(res_ref[pl.ds(local, 1), :], (8, res_ref.shape[1]))
            term = jnp.dot(row.astype(BF16), interp_ref[local], preferred_element_type=F32)
            col_ref[pl.ds(local, 1), :] = term[0:1]
        return carry

    lax.fori_loop(0, count // unroll, back, 0)


def bend_kernel(
    group,
    unroll,
    corner_ref,
    planes_ref,
    kh_ref,
    kl_ref,
    y_ref,
    row_ref,
    prob_ref,
    interp_ref,
    out_ref,
    image,
):
    step = pl.program_id(0)
    count = interp_ref.shape[0]
    size_x = image.shape[1]

    @pl.when(step == 0)
    def _():
        mix_depth(planes_ref, kh_ref, kl_ref, image, group, size_x)

    def some(part, carry):
        for k in range(unroll):
            local = part * unroll + k
            values = pick_values(
                image, corner_ref, y_ref, row_ref, step * count + local, local, 1
            )
            bend = lax.dot_general(values, interp_ref[local], NT, preferred_element_type=F32)
            out_ref[pl.ds(local, 1), :] = bend[0:1]
        return carry

    lax.fori_loop(0, count // unroll, some, 0)
    prob = prob_ref[...]
    out_ref[...] = prob * (1.0 - prob) * out_ref[...]


def scatter_kernel(slab, unroll, ids_ref, count_ref, z_ref, y_ref, key_ref, term_ref, out_ref):
    cols = y_ref.shape[-1]
    size_y = out_ref.shape[-1]
    rows = BOXZ * slab
    out_ref[...] = jnp.zeros_like(out_ref)

    def some(part, carry):
        sums = []
        for k in range(unroll):
            block = ids_ref[part * unroll + k]
            row_line = lax.broadcasted_iota(jnp.int32, (rows, cols), 0)
            y_line = lax.broadcasted_iota(jnp.int32, (size_y, cols), 0)
            wanted = row_line == key_ref[pl.ds(block, 1), :]
            left = jnp.where(wanted, term_ref[pl.ds(block, 1), :], 0.0).astype(BF16)
            right = jnp.where(y_line == y_ref[pl.ds(block, 1), :], 1.0, 0.0).astype(BF16)
            sums.append((block, lax.dot_general(left, right, NT, preferred_element_type=F32)))
        for block, piece in sums:
            at = pl.multiple_of(z_ref[block] * slab, slab)
            out_ref[pl.ds(at, rows), :] += piece
        return carry

    lax.fori_loop(0, lax.div(count_ref[0] + unroll - 1, unroll), some, 0)


def whole(shape):
    return pl.BlockSpec(
        shape, lambda i, *_: (0,) * len(shape), pipeline_mode=pl.Buffered(buffer_count=1)
    )


def params():
    return pltpu.CompilerParams(
        vmem_limit_bytes=VMEM_BYTES, dimension_semantics=("arbitrary",)
    )


def body(
    grid_weights,
    direction,
    kern_x,
    kern_y,
    kern_z,
    interp,
    block_corner,
    block_offsets,
    labels,
    trial_steps,
    accept,
):
    slab, size_y, size_z = grid_weights.shape
    size_x = kern_x.shape[0]
    devices = lax.axis_size("pts")
    me = lax.axis_index("pts")
    blocks, cols = block_offsets.shape
    per_block = interp.shape[1]
    points = blocks * per_block * devices
    group = max(1, PACK // slab)
    pack = group * slab
    unroll = 4
    count = 16

    spare = jnp.pad(block_corner, ((0, PACK - 3), (0, cols - blocks)))
    sent = jnp.concatenate([block_offsets, spare], axis=0).astype(jnp.int16)
    everyone = lax.all_gather(sent, "pts", axis=0)

    planes = plane_mix(jnp.stack([grid_weights, direction]), kern_y, kern_z)
    planes = planes.reshape(size_z * 2 // group, pack, size_y)
    gathered = lax.all_gather(planes, "pts", axis=0)
    kern_high, kern_low = widen_kern(kern_x, devices, slab, group)

    y_cell = block_corner[1][:, None] + block_offsets // BOXZ % BOXY
    box_row = block_offsets % BOXZ * BOXX + block_offsets // (BOXY * BOXZ)
    chosen = jnp.sum(jnp.where(jnp.arange(NTRIAL) == accept[0], trial_steps, 0.0))

    steps = blocks // count
    rows_of = lambda width: pl.BlockSpec((count, width), lambda i, *_: (i, 0))
    interp_spec = pl.BlockSpec((count, per_block, cols), lambda i, *_: (i, 0, 0))
    pair, probability, column_term, own = pl.pallas_call(
        functools.partial(forward_kernel, group, unroll),
        grid_spec=pltpu.PrefetchScalarGridSpec(
            num_scalar_prefetch=3,
            grid=(steps,),
            in_specs=[
                whole(gathered.shape),
                whole(kern_high.shape),
                whole(kern_low.shape),
                rows_of(cols),
                rows_of(cols),
                rows_of(per_block),
                interp_spec,
            ],
            out_specs=[
                pl.BlockSpec((2, count, per_block), lambda i, *_: (0, i, 0)),
                rows_of(per_block),
                rows_of(cols),
                pl.BlockSpec((2 * size_z, slab, size_y), lambda i, *_: (0, 0, 0)),
            ],
            scratch_shapes=[
                pltpu.VMEM((2 * size_z, size_x, size_y), F32),
                pltpu.VMEM((count, per_block), F32),
            ],
        ),
        out_shape=[
            jax.ShapeDtypeStruct((2, blocks, per_block), F32),
            jax.ShapeDtypeStruct((blocks, per_block), F32),
            jax.ShapeDtypeStruct((blocks, cols), F32),
            jax.ShapeDtypeStruct((2 * size_z, slab, size_y), F32),
        ],
        compiler_params=params(),
        name="forward",
    )(
        block_corner,
        me.astype(jnp.int32).reshape(1),
        chosen.reshape(1),
        gathered,
        kern_high,
        kern_low,
        y_cell,
        box_row,
        labels,
        interp,
    )

    terms = lax.all_gather(column_term.astype(BF16), "pts", axis=0, tiled=True).astype(F32)

    far_offsets = everyone[:, :blocks].astype(jnp.int32).reshape(devices * blocks, cols)
    far = everyone[:, blocks : blocks + 3, :blocks].astype(jnp.int32)
    far_x, far_y, far_z = (far[:, k].reshape(-1) for k in range(3))
    x_from = far_x - me * slab
    far_cell = x_from[:, None] + far_offsets // (BOXY * BOXZ)
    inside = (far_cell >= 0) & (far_cell < slab)
    key = jnp.where(inside, far_offsets % BOXZ * slab + far_cell, -1)
    far_line = far_y[:, None] + far_offsets // BOXZ % BOXY
    total = devices * blocks
    touches = (x_from < slab) & (x_from > -BOXX)
    ranks = jnp.arange(total, dtype=jnp.int32)
    ids = lax.sort(jnp.where(touches, ranks, ranks + total))
    ids = jnp.where(ids >= total, ids - total, ids)
    touched = jnp.sum(touches.astype(jnp.int32)).reshape(1)

    spread = pl.pallas_call(
        functools.partial(scatter_kernel, slab, unroll),
        grid_spec=pltpu.PrefetchScalarGridSpec(
            num_scalar_prefetch=3,
            grid=(1,),
            in_specs=[whole((total, cols))] * 3,
            out_specs=pl.BlockSpec((size_z * slab, size_y), lambda i, *_: (0, 0)),
        ),
        out_shape=jax.ShapeDtypeStruct((size_z * slab, size_y), F32),
        compiler_params=params(),
        name="spread",
    )(ids, touched, far_z, far_line, key, terms)

    new_weights = grid_weights + chosen * direction
    grid_gradient = (
        jnp.transpose(spread.reshape(size_z, slab, size_y), (1, 2, 0)) - new_weights
    )

    fields = own.reshape(size_z, 2, slab, size_y)
    weights_t = jnp.transpose(grid_weights, (2, 0, 1))
    direction_t = jnp.transpose(direction, (2, 0, 1))
    quads = jnp.stack(
        [
            jnp.sum(weights_t * fields[:, 0]),
            jnp.sum(direction_t * fields[:, 0]),
            jnp.sum(direction_t * fields[:, 1]),
        ]
    )
    latent, slope_pt = pair[0], pair[1]
    target = labels.astype(F32)
    signed = 2.0 * target - 1.0
    trial_latent = latent[None] + trial_steps[:, None, None] * slope_pt[None]
    loglik = jnp.sum(jax.nn.log_sigmoid(signed[None] * trial_latent), axis=(1, 2))
    descent = jnp.sum(
        (target[None] - jax.nn.sigmoid(trial_latent)) * slope_pt[None], axis=(1, 2)
    )
    sums = jnp.concatenate([loglik, descent, quads])
    first = high_part(sums)
    second = high_part(sums - first)
    third = sums - first - second
    split = jnp.stack([first, second, third]).astype(BF16)
    split = jnp.pad(split, ((0, pack - 3), (0, size_y - split.shape[1])))

    bend_planes = plane_mix(grid_gradient[None], kern_y, kern_z)
    bend_planes = bend_planes.reshape(size_z // group, pack, size_y)
    bend_sent = jnp.concatenate([bend_planes, split[None], split[None]], axis=0)
    bend_all = lax.all_gather(bend_sent, "pts", axis=0)
    units = size_z // group

    curvature = pl.pallas_call(
        functools.partial(bend_kernel, group, unroll),
        grid_spec=pltpu.PrefetchScalarGridSpec(
            num_scalar_prefetch=1,
            grid=(steps,),
            in_specs=[
                whole((devices, units, pack, size_y)),
                whole(kern_high.shape),
                whole(kern_low.shape),
                rows_of(cols),
                rows_of(cols),
                rows_of(per_block),
                interp_spec,
            ],
            out_specs=rows_of(per_block),
            scratch_shapes=[pltpu.VMEM((size_z, size_x, size_y), F32)],
        ),
        out_shape=jax.ShapeDtypeStruct((blocks, per_block), F32),
        compiler_params=params(),
        name="bend",
    )(
        block_corner,
        bend_all,
        kern_high,
        kern_low,
        y_cell,
        box_row,
        probability,
        interp,
    )

    got = bend_all[:, units, :3, : sums.shape[0]].astype(F32)
    everything = jnp.sum(got, axis=(0, 1))
    loglik = everything[:NTRIAL]
    descent = everything[NTRIAL : 2 * NTRIAL]
    quad_gu, quad_du, quad_dv = (everything[2 * NTRIAL + k] for k in range(3))
    prior = 0.5 * (quad_gu + 2.0 * trial_steps * quad_du + trial_steps * trial_steps * quad_dv)
    trial_objective = (loglik - prior) / points
    trial_slope = (descent - quad_du - trial_steps * quad_dv) / points
    return (new_weights, grid_gradient, curvature, trial_objective, trial_slope)


def solution(mesh):
    return jax.shard_map(
        body,
        mesh=mesh,
        in_specs=(
            P(("parts", "pts"), None, None),
            P(("parts", "pts"), None, None),
            P(),
            P(),
            P(),
            P(("parts", "pts"), None, None),
            P(None, ("parts", "pts")),
            P(("parts", "pts"), None),
            P(("parts", "pts"), None),
            P(),
            P(),
        ),
        out_specs=(
            P(("parts", "pts"), None, None),
            P(("parts", "pts"), None, None),
            P(("parts", "pts"), None),
            P("parts"),
            P("parts"),
        ),
        check_vma=False,
    )
```

time: 989 us -> 316 us (0.32)
  local copies, waits for them, and re-layouts: 382 us -> 8.23 us
  other arithmetic: 338 us -> 26.3 us
  Pallas kernels: 0 us -> 95.7 us
  waiting for transfers between devices: 174 us -> 134 us
  matrix products: 41.3 us -> 5.56 us
    gather x2 -> x0, local copies, waits for them, and re-layouts: 327 us -> none  [pick_cells(): taken = jnp.take(grid_rows, row_ids, axis=1)]
    scatter-add x1 -> x0, other arithmetic: 199 us -> none  [slab_add(): jnp.zeros((row_count * size_y, size_z), jnp.float32).at[target_row]]
    reduce_sum x3 -> x2, other arithmetic: 115 us -> 1.78 us  [the longest x1 0.99 us: body(): jnp.sum(direction_t * fields[:, 1])]
    reduce_scatter x1 -> x0, waiting for transfers between devices: 102 us -> none  [body(): lax.psum_scatter(slab_add(flat_rows, flat_depths, flat_terms, slab_rows *...]
    pallas_call x0 -> x3, Pallas kernels: none -> 95.7 us  [the longest x1 57.2 us: body(): pl.pallas_call(functools.partial(forward_kernel, group, unroll), grid_spe...]
    all_gather x2 -> x3, waiting for transfers between devices: 72.2 us -> 134 us  [the longest x1 69 us: body(): bend_all = lax.all_gather(bend_sent, 'pts', axis=0)]
    dot_general x9 -> x4, matrix products: 41.3 us -> 5.56 us  [the longest x2 2.8 us: plane_mix(): jnp.einsum('zfab,yb->zfay', inner, kern_y, precision=HIGHEST).astype(BF16)]
    psum x1 -> x0, blocking collectives: 33.4 us -> none  [body(): loglik, descent = lax.psum((loglik_local, descent_local), 'pts')]
  transfers between devices with their start and end apart: 3 -> 3, of which waited for: 3 -> 3; matrix products, arithmetic and copies ran while one was open for 2% -> 7% of each run, Pallas kernels for 0% -> 0%
where the time goes in v1:
time: 316 us
  waiting for transfers between devices  134 us (42%)
  Pallas kernels  95.7 us (30%)
  blocking collectives  31.1 us (10%)
  other arithmetic  26.3 us (8%)
  between operations  15.3 us (5%)
  local copies, waits for them, and re-layouts  8.23 us (3%)
  matrix products  5.56 us (2%)
    all_gather x1, waiting for transfers between devices, body(): bend_all = lax.all_gather(bend_sent, 'pts', axis=0)  69 us
    pallas_call x1, Pallas kernels, body(): pl.pallas_call(functools.partial(forward_kernel, group, unroll), grid_spe...  57.2 us
    all_gather x1, waiting for transfers between devices, body(): gathered = lax.all_gather(planes, 'pts', axis=0)  39.4 us
    all_gather x1, blocking collectives, body(): everyone = lax.all_gather(sent, 'pts', axis=0)  31.1 us
    all_gather x1, waiting for transfers between devices, body(): lax.all_gather(column_term.astype(BF16), 'pts', axis=0, tiled=True)  25.4 us
    pallas_call x1, Pallas kernels, body(): pl.pallas_call(functools.partial(bend_kernel, group, unroll), grid_spec=p...  24.1 us
    pallas_call x1, Pallas kernels, body(): pl.pallas_call(functools.partial(scatter_kernel, slab, unroll), grid_spec...  14.3 us
  transfers between devices with their start and end apart: 3, of which 3 were waited for; matrix products, arithmetic and copies ran while one was open for 7% of the time, Pallas kernels for 0%

profile of v1, /device:TPU:0, one launch (start us, length us, event | category | flops | bytes accessed | tf_op | source)
XLA Modules:
  0.0 316.2 jit_solution(16299393635825418411)
XLA Ops:
  7.2 0.8 copy-done
  8.0 2.2 convolution_bitcast_fusion
  10.2 1.8 convolution_convert_fusion
  12.1 1.1 copy.39
  14.4 0.9 fusion.25
  15.4 31.1 %all-gather.11 = s16[16,144,256]{2,1,0:T(8,128)(2,1)S(1)} all-gather(s16[1,144,256]{2,1,0:T(8,128)(2,1)S(1)} %pad_add_fusion), channel_id=1, replica_groups=mesh['parts'=2,'pts'=16] {'pts'}, dimensions={0}, use_global_device_ids=true | all-gather | bytes 1253376 | tf_op jit(solution)/shard_map/all_gather | solution.py:243
  46.6 0.7 fusion.47
  47.3 1.2 fusion.50
  48.6 0.7 fusion.21
  49.3 5.7 %fusion.10 = (s32[2048,256]{1,0:T(8,128)}, s32[2048,256]{1,0:T(8,128)}) fusion(s16[16,128,256]{2,1,0:T(8,128)(2,1)S(1)} %slice.69, s32[2048]{0:T(1024)S(1)} %bitcast.105, s32[2048]{0:T(1024)S(1)} %bitcast.108), kind=kLoop, calls=%fused_computation.24 | loop fusion | flops 25690112 | bytes 5259264 | tf_op jit(solution)/shard_map/jit(_where)/select_n | solution.py:311
  54.9 39.4 %all-gather.6.cloned.1.call-done.planes_ref = bf16[16,128,16,128]{3,2,1,0:T(8,128)(2,1)} async-done(((bf16[1,128,16,128]{3,2,1,0:T(8,128)(2,1)}), bf16[16,128,16,128]{3,2,1,0:T(8,128)(2,1)}) %all-gather.6.cloned.1.call-update) | async-done | bytes 8388624 | tf_op jit(solution)/shard_map/all_gather | solution.py:247
  94.3 57.2 %forward.1 = (f32[2,128,128]{2,1,0:T(8,128)}, f32[128,128]{1,0:T(8,128)}, f32[128,256]{1,0:T(8,128)}, f32[256,8,128]{2,1,0:T(8,128)}) custom-call(s32[3,128]{1,0:T(4,128)} %corner_ref.3, s32[1]{0:T(128)} %bitcast.9.slab_ref, f32[1]{0:T(128)} %bitcast.10.chosen_ref, bf16[16,128,16,128]{3,2,1,0:T(8,128)(2,1)} %all-gather.6.cloned.1.call-done.planes_ref, ...), custom_call_target="tpu_custom_call" | custom-call | tf_op jit(solution)/shard_map/forward/pallas_call | solution.py:257
  151.6 1.5 convert_element_type.58
  153.3 5.0 %sort.14 = (s32[2048]{0:T(1024)S(1)}, s32[2048]{0:T(1024)}) sort(s32[2048]{0:T(1024)S(1)} %add_select_fusion.8, s32[2048]{0:T(1024)S(1)} %iota.28), dimensions={0}, to_apply=%region_1.2 | sort | flops 22528 | bytes 32768 | tf_op jit(solution)/shard_map/sort | solution.py:316
  158.3 0.6 compare_select_fusion.1.ids_ref
  158.9 1.4 fusion.49
  160.8 0.5 multiply_reduce_fusion
  161.3 1.0 fusion.17
  162.3 2.0 concatenate.63
  164.3 25.4 %all-gather.8.cloned.1.call-done = bf16[2048,256]{1,0:T(8,128)(2,1)} async-done(((bf16[128,256]{1,0:T(8,128)(2,1)}), bf16[2048,256]{1,0:T(8,128)(2,1)}) %all-gather.8.cloned.1.call-update) | async-done | bytes 1048592 | tf_op jit(solution)/shard_map/all_gather | solution.py:303
  189.8 2.7 convert_element_type.59.term_ref
  192.5 14.3 %spread.1 = f32[1024,128]{1,0:T(8,128)} custom-call(s32[2048]{0:T(1024)} %compare_select_fusion.1.ids_ref, s32[1]{0:T(128)} %bitcast.4.count_ref, s32[2048]{0:T(1024)} %bitcast.107, s32[2048,256]{1,0:T(8,128)} %get-tuple-element.28.y_ref, s32[2048,256]{1,0:T(8,128)} %get-tuple-element.27.key_ref, f32[2048,256]{1,0:T(8,128)} %convert_element_type.59.term_ref), custom_call_target="tpu_custom_call" | custom-call | tf_op jit(solution)/shard_map/spread/pallas_call | solution.py:320
  206.8 1.2 copy.43
  208.1 1.6 bitcast_subtract_fusion
  209.6 0.6 convolution_bitcast_fusion.1
  210.2 1.0 convolution_convert_fusion.1
  211.4 0.7 pad_maximum_fusion
  212.2 69.0 %all-gather.10.cloned.1.call-done = bf16[1056,16,128]{2,1,0:T(8,128)(2,1)} async-done(((bf16[66,16,128]{2,1,0:T(8,128)(2,1)}), bf16[1056,16,128]{2,1,0:T(8,128)(2,1)}) %all-gather.10.cloned.1.call-update) | async-done | bytes 4325392 | tf_op jit(solution)/shard_map/all_gather | solution.py:366
  281.1 0.8 convert_reduce_fusion
  281.9 0.6 fusion.51
  282.6 24.1 %bend.1 = f32[128,128]{1,0:T(8,128)} custom-call(s32[3,128]{1,0:T(4,128)} %corner_ref.3, bf16[16,66,16,128]{3,2,1,0:T(8,128)(2,1)} %bitcast.97, bf16[256,256]{1,0:T(8,128)(2,1)} %get-tuple-element.30.kh_ref, bf16[256,256]{1,0:T(8,128)(2,1)} %get-tuple-element.29.kl_ref, s32[128,256]{1,0:T(8,128)} %get-tuple-element.35.y_ref, ...), custom_call_target="tpu_custom_call" | custom-call | tf_op jit(solution)/shard_map/bend/pallas_call | solution.py:369
  307.3 2.4 subtract_multiply_fusion
  (49 shorter events, 1.5 us)
Async XLA Ops:
  7.2 0.8 copy-start
  7.2 3.0 copy-start.5
  7.2 87.2 %all-gather.6.cloned.1.call-start = ((), (), s32[]{:S(2)}) async-start(), calls=%async_computation | async-start | bytes 8912896 | tf_op jit(solution)/shard_map/all_gather | solution.py:247
  10.2 3.1 copy-start.8
  10.2 4.2 %copy-start.9 = (s32[3,128]{1,0:T(4,128)S(1)}, s32[3,128]{1,0:T(4,128)}, u32[]{:S(2)}) copy-start(s32[3,128]{1,0:T(4,128)} %corner_ref.3) | copy-start | bytes 4612
  10.2 4.2 %copy-start.7 = (s32[128,256]{1,0:T(8,128)S(1)}, s32[128,256]{1,0:T(8,128)}, u32[]{:S(2)}) copy-start(s32[128,256]{1,0:T(8,128)} %param.18) | copy-start | bytes 393220
  13.2 176.6 %all-gather.8.cloned.1.call-start = ((), (), s32[]{:S(2)}) async-start(), calls=%async_computation.1 | async-start | bytes 1114112 | tf_op jit(solution)/shard_map/all_gather | solution.py:303
  13.7 32.9 %copy-start.10 = (f32[5]{0:T(128)S(1)}, f32[5]{0:T(128)}, u32[]{:S(2)}) copy-start(f32[5]{0:T(128)} %param.20) | copy-start | bytes 64
  94.3 58.9 %copy-start.4 = (s32[128,128]{1,0:T(8,128)S(1)}, s32[128,128]{1,0:T(8,128)}, u32[]{:S(2)}) copy-start(s32[128,128]{1,0:T(8,128)} %labels_ref.1) | copy-start | bytes 196612
  153.2 128.0 %all-gather.10.cloned.1.call-start = ((), (), s32[]{:S(2)}) async-start(), calls=%async_computation.2 | async-start | bytes 4595712 | tf_op jit(solution)/shard_map/all_gather | solution.py:366
  158.9 1.9 copy-start.6
  158.9 2.4 copy-start.1
  158.9 2.4 copy-start.2
  209.6 97.1 %copy-start.3 = (f32[8,128,128]{2,1,0:T(8,128)}, f32[8,128,128]{2,1,0:T(8,128)S(1)}, u32[]{:S(2)}) copy-start(f32[8,128,128]{2,1,0:T(8,128)S(1)} %get-tuple-element.21) | copy-start | bytes 1572868
Sparse Core Ops, SparseCore 0:
  13.3 80.9 all-gather.5
  153.3 36.4 all-gather.7
  212.3 68.7 all-gather.9

commit v2 on v1

--- a/solution.py
+++ b/solution.py
@@ -6,6 +6,7 @@
 from jax.experimental import pallas as pl
 from jax.experimental.pallas import tpu as pltpu
 from jax.sharding import PartitionSpec as P
+
 
 BOXX = 16
 BOXY = 16
@@ -81,6 +82,45 @@
     return stacked.astype(BF16)
 
 
+def latent_kernel(
+    group,
+    unroll,
+    corner_ref,
+    slab_ref,
+    planes_ref,
+    kh_ref,
+    kl_ref,
+    y_ref,
+    row_ref,
+    interp_ref,
+    latent_ref,
+    own_ref,
+    image,
+):
+    step = pl.program_id(0)
+    count = interp_ref.shape[0]
+    size_x = image.shape[1]
+
+    @pl.when(step == 0)
+    def _():
+        mix_depth(planes_ref, kh_ref, kl_ref, image, group, size_x)
+        slab = own_ref.shape[1]
+        at = pl.multiple_of(slab_ref[0] * slab, slab)
+        own_ref[...] = image[:, pl.ds(at, slab), :]
+
+    def some(part, carry):
+        for k in range(unroll):
+            local = part * unroll + k
+            values = pick_values(
+                image, corner_ref, y_ref, row_ref, step * count + local, local, 1
+            )
+            line = lax.dot_general(values, interp_ref[local], NT, preferred_element_type=F32)
+            latent_ref[pl.ds(local, 1), :] = line[0:1]
+        return carry
+
+    lax.fori_loop(0, count // unroll, some, 0)
+
+
 def forward_kernel(
     group,
     unroll,
@@ -93,13 +133,15 @@
     y_ref,
     row_ref,
     labels_ref,
+    latent_ref,
     interp_ref,
-    latent_ref,
+    slope_ref,
     prob_ref,
     col_ref,
     own_ref,
     image,
     res_ref,
+    term_ref,
 ):
     step = pl.program_id(0)
     count = interp_ref.shape[0]
@@ -116,15 +158,14 @@
         for k in range(unroll):
             local = part * unroll + k
             values = pick_values(
-                image, corner_ref, y_ref, row_ref, step * count + local, local, 2
+                image, corner_ref, y_ref, row_ref, step * count + local, local, 1
             )
-            pair = lax.dot_general(values, interp_ref[local], NT, preferred_element_type=F32)
-            latent_ref[0, pl.ds(local, 1), :] = pair[0:1]
-            latent_ref[1, pl.ds(local, 1), :] = pair[1:2]
+            line = lax.dot_general(values, interp_ref[local], NT, preferred_element_type=F32)
+            slope_ref[pl.ds(local, 1), :] = line[0:1]
         return carry
 
     lax.fori_loop(0, count // unroll, some, 0)
-    logits = latent_ref[0] + chosen_ref[0] * latent_ref[1]
+    logits = latent_ref[...] + chosen_ref[0] * slope_ref[...]
     prob = jax.nn.sigmoid(logits)
     prob_ref[...] = prob
     res_ref[...] = (labels_ref[...].astype(F32) - prob).astype(BF16).astype(F32)
@@ -134,10 +175,11 @@
             local = part * unroll + k
             row = jnp.broadcast_to(res_ref[pl.ds(local, 1), :], (8, res_ref.shape[1]))
             term = jnp.dot(row.astype(BF16), interp_ref[local], preferred_element_type=F32)
-            col_ref[pl.ds(local, 1), :] = term[0:1]
+            term_ref[pl.ds(local, 1), :] = term[0:1]
         return carry
 
     lax.fori_loop(0, count // unroll, back, 0)
+    col_ref[...] = term_ref[...].astype(BF16)
 
 
 def bend_kernel(
@@ -235,16 +277,19 @@
     points = blocks * per_block * devices
     group = max(1, PACK // slab)
     pack = group * slab
-    unroll = 4
+    unroll = 8
     count = 16
 
     spare = jnp.pad(block_corner, ((0, PACK - 3), (0, cols - blocks)))
     sent = jnp.concatenate([block_offsets, spare], axis=0).astype(jnp.int16)
+    units = size_z // group
+    sides = []
+    for field in (grid_weights, direction):
+        planes = plane_mix(field[None], kern_y, kern_z).reshape(units, pack, size_y)
+        sides.append(lax.all_gather(planes, "pts", axis=0))
+    gathered_w, gathered_d = sides
+    gathered_w, sent = lax.optimization_barrier((gathered_w, sent))
     everyone = lax.all_gather(sent, "pts", axis=0)
-
-    planes = plane_mix(jnp.stack([grid_weights, direction]), kern_y, kern_z)
-    planes = planes.reshape(size_z * 2 // group, pack, size_y)
-    gathered = lax.all_gather(planes, "pts", axis=0)
     kern_high, kern_low = widen_kern(kern_x, devices, slab, group)
 
     y_cell = block_corner[1][:, None] + block_offsets // BOXZ % BOXY
@@ -254,53 +299,86 @@
     steps = blocks // count
     rows_of = lambda width: pl.BlockSpec((count, width), lambda i, *_: (i, 0))
     interp_spec = pl.BlockSpec((count, per_block, cols), lambda i, *_: (i, 0, 0))
-    pair, probability, column_term, own = pl.pallas_call(
+    work = pl.CostEstimate(
+        flops=4 * blocks * size_y * size_y * cols,
+        bytes_accessed=gathered_w.size * 2 + interp.size * 2,
+        transcendentals=0,
+    )
+    mine = me.astype(jnp.int32).reshape(1)
+    own_spec = pl.BlockSpec((size_z, slab, size_y), lambda i, *_: (0, 0, 0))
+    own_shape = jax.ShapeDtypeStruct((size_z, slab, size_y), F32)
+    point_shape = jax.ShapeDtypeStruct((blocks, per_block), F32)
+    image_scratch = pltpu.VMEM((size_z, size_x, size_y), F32)
+    latent, own_w = pl.pallas_call(
+        functools.partial(latent_kernel, group, unroll),
+        grid_spec=pltpu.PrefetchScalarGridSpec(
+            num_scalar_prefetch=2,
+            grid=(steps,),
+            in_specs=[
+                whole(gathered_w.shape),
+                whole(kern_high.shape),
+                whole(kern_low.shape),
+                rows_of(cols),
+                rows_of(cols),
+                interp_spec,
+            ],
+            out_specs=[rows_of(per_block), own_spec],
+            scratch_shapes=[image_scratch],
+        ),
+        out_shape=[point_shape, own_shape],
+        compiler_params=params(),
+        cost_estimate=work,
+        name="latent",
+    )(block_corner, mine, gathered_w, kern_high, kern_low, y_cell, box_row, interp)
+
+    forward = pl.pallas_call(
         functools.partial(forward_kernel, group, unroll),
         grid_spec=pltpu.PrefetchScalarGridSpec(
             num_scalar_prefetch=3,
             grid=(steps,),
             in_specs=[
-                whole(gathered.shape),
+                whole(gathered_d.shape),
                 whole(kern_high.shape),
                 whole(kern_low.shape),
                 rows_of(cols),
                 rows_of(cols),
+                rows_of(per_block),
                 rows_of(per_block),
                 interp_spec,
             ],
             out_specs=[
-                pl.BlockSpec((2, count, per_block), lambda i, *_: (0, i, 0)),
                 rows_of(per_block),
-                rows_of(cols),
-                pl.BlockSpec((2 * size_z, slab, size_y), lambda i, *_: (0, 0, 0)),
+                rows_of(per_block),
+                rows_of(cols),
+                own_spec,
             ],
-            scratch_shapes=[
-                pltpu.VMEM((2 * size_z, size_x, size_y), F32),
-                pltpu.VMEM((count, per_block), F32),
-            ],
+            scratch_shapes=[image_scratch, pltpu.VMEM((count, per_block), F32), pltpu.VMEM((count, cols), F32)],
         ),
         out_shape=[
-            jax.ShapeDtypeStruct((2, blocks, per_block), F32),
-            jax.ShapeDtypeStruct((blocks, per_block), F32),
-            jax.ShapeDtypeStruct((blocks, cols), F32),
-            jax.ShapeDtypeStruct((2 * size_z, slab, size_y), F32),
+            point_shape,
+            point_shape,
+            jax.ShapeDtypeStruct((blocks, cols), BF16),
+            own_shape,
         ],
         compiler_params=params(),
+        cost_estimate=work,
         name="forward",
-    )(
+    )
+    slope_pt, probability, column_term, own_d = forward(
         block_corner,
-        me.astype(jnp.int32).reshape(1),
+        mine,
         chosen.reshape(1),
-        gathered,
+        gathered_d,
         kern_high,
         kern_low,
         y_cell,
         box_row,
         labels,
+        latent,
         interp,
     )
 
-    terms = lax.all_gather(column_term.astype(BF16), "pts", axis=0, tiled=True).astype(F32)
+    terms = lax.all_gather(column_term, "pts", axis=0, tiled=True).astype(F32)
 
     far_offsets = everyone[:, :blocks].astype(jnp.int32).reshape(devices * blocks, cols)
     far = everyone[:, blocks : blocks + 3, :blocks].astype(jnp.int32)
@@ -335,17 +413,15 @@
         jnp.transpose(spread.reshape(size_z, slab, size_y), (1, 2, 0)) - new_weights
     )
 
-    fields = own.reshape(size_z, 2, slab, size_y)
     weights_t = jnp.transpose(grid_weights, (2, 0, 1))
     direction_t = jnp.transpose(direction, (2, 0, 1))
     quads = jnp.stack(
         [
-            jnp.sum(weights_t * fields[:, 0]),
-            jnp.sum(direction_t * fields[:, 0]),
-            jnp.sum(direction_t * fields[:, 1]),
+            jnp.sum(weights_t * own_w),
+            jnp.sum(direction_t * own_w),
+            jnp.sum(direction_t * own_d),
         ]
     )
-    latent, slope_pt = pair[0], pair[1]
     target = labels.astype(F32)
     signed = 2.0 * target - 1.0
     trial_latent = latent[None] + trial_steps[:, None, None] * slope_pt[None]
@@ -364,8 +440,6 @@
     bend_planes = bend_planes.reshape(size_z // group, pack, size_y)
     bend_sent = jnp.concatenate([bend_planes, split[None], split[None]], axis=0)
     bend_all = lax.all_gather(bend_sent, "pts", axis=0)
-    units = size_z // group
-
     curvature = pl.pallas_call(
         functools.partial(bend_kernel, group, unroll),
         grid_spec=pltpu.PrefetchScalarGridSpec(

time: 316 us -> 293 us (0.927)
  Pallas kernels: 95.7 us -> 77 us
  blocking collectives: 31.1 us -> 25.1 us
    pallas_call x1 -> x2, Pallas kernels: 57.2 us -> 45.5 us  [the longest x1 24.5 us: body(): forward(block_corner, mine, chosen.reshape(1), gathered_d, kern_high, ker...]
    all_gather x2 -> x3, waiting for transfers between devices: 64.8 us -> 73.4 us  [the longest x2 54.4 us: body(): sides.append(lax.all_gather(planes, 'pts', axis=0))]
    all_gather x1, waiting for transfers between devices: 69 us -> 60.4 us  [body(): bend_all = lax.all_gather(bend_sent, 'pts', axis=0)]
    all_gather x1, blocking collectives: 31.1 us -> 25.1 us  [body(): everyone = lax.all_gather(sent, 'pts', axis=0)]
    pallas_call x1, Pallas kernels: 14.3 us -> 10.8 us  [body(): pl.pallas_call(functools.partial(scatter_kernel, slab, unroll), grid_spec...]
    pallas_call x1, Pallas kernels: 24.1 us -> 20.7 us  [body(): pl.pallas_call(functools.partial(bend_kernel, group, unroll), grid_spec=p...]
  transfers between devices with their start and end apart: 3 -> 4, of which waited for: 3 -> 4; matrix products, arithmetic and copies ran while one was open for 7% -> 8% of each run, Pallas kernels for 0% -> 7%
where the time goes in v2:
time: 293 us; the launch traced here: 292 us
  waiting for transfers between devices  134 us (46%)
  Pallas kernels  77 us (26%)
  other arithmetic  26.5 us (9%)
  blocking collectives  25.1 us (9%)
  between operations  15.2 us (5%)
  local copies, waits for them, and re-layouts  8.34 us (3%)
  matrix products  5.84 us (2%)
    all_gather x1, waiting for transfers between devices, body(): bend_all = lax.all_gather(bend_sent, 'pts', axis=0)  60.4 us
    all_gather x2, waiting for transfers between devices, body(): sides.append(lax.all_gather(planes, 'pts', axis=0))  54.4 us
    all_gather x1, blocking collectives, body(): everyone = lax.all_gather(sent, 'pts', axis=0)  25.1 us
    pallas_call x1, Pallas kernels, body(): forward(block_corner, mine, chosen.reshape(1), gathered_d, kern_high, ker...  24.5 us
    pallas_call x1, Pallas kernels, body(): pl.pallas_call(functools.partial(latent_kernel, group, unroll), grid_spec...  21 us
    pallas_call x1, Pallas kernels, body(): pl.pallas_call(functools.partial(bend_kernel, group, unroll), grid_spec=p...  20.7 us
    all_gather x1, waiting for transfers between devices, body(): terms = lax.all_gather(column_term, 'pts', axis=0, tiled=True).astype(F32)  19.1 us
    pallas_call x1, Pallas kernels, body(): pl.pallas_call(functools.partial(scatter_kernel, slab, unroll), grid_spec...  10.8 us
  transfers between devices with their start and end apart: 4, of which 4 were waited for; matrix products, arithmetic and copies ran while one was open for 8% of the time, Pallas kernels for 7%

profile of v2, /device:TPU:0, one launch (start us, length us, event | category | flops | bytes accessed | tf_op | source)
XLA Modules:
  0.0 292.2 jit_solution(95594807841656086)
XLA Ops:
  7.2 0.8 copy-done
  8.0 1.6 fusion.34
  9.6 1.5 convolution_convert_fusion.2
  11.1 0.9 copy.48
  13.3 0.9 copy.49
  14.5 1.0 copy.57
  16.7 0.6 fusion.48
  17.3 0.9 fusion.22
  18.3 0.8 fusion.18
  19.1 46.2 %all-gather.8.cloned.1.call-done.planes_ref = bf16[16,64,16,128]{3,2,1,0:T(8,128)(2,1)} async-done(((bf16[1,64,16,128]{3,2,1,0:T(8,128)(2,1)}), bf16[16,64,16,128]{3,2,1,0:T(8,128)(2,1)}) %all-gather.8.cloned.1.call-update) | async-done | bytes 4194320 | tf_op jit(solution)/shard_map/all_gather | solution.py:289
  65.3 25.1 %all-gather.15 = s16[2304,256]{1,0:T(8,128)(2,1)S(1)} all-gather(s16[144,256]{1,0:T(8,128)(2,1)S(1)} %pad_add_fusion), channel_id=2, replica_groups=mesh['parts'=2,'pts'=16] {'pts'}, dimensions={0}, use_global_device_ids=true | all-gather | bytes 1253376 | tf_op jit(solution)/shard_map/all_gather | solution.py:292
  90.5 21.0 %latent.1 = (f32[128,128]{1,0:T(8,128)}, f32[128,8,128]{2,1,0:T(8,128)}) custom-call(s32[3,128]{1,0:T(4,128)} %corner_ref.5, s32[1]{0:T(128)} %bitcast.11.slab_ref, bf16[16,64,16,128]{3,2,1,0:T(8,128)(2,1)} %all-gather.8.cloned.1.call-done.planes_ref, bf16[256,256]{1,0:T(8,128)(2,1)} %get-tuple-element.36.kh_ref, bf16[256,256]{1,0:T(8,128)(2,1)} %get-tuple-element.35.kl_ref, ...), custom_call_target="tpu_custom_call" | custom-call | flops 2147483648 | bytes 12582912 | tf_op jit(solution)/shard_map/latent/pallas_call | solution.py:312
  111.5 8.2 %all-gather.10.cloned.1.call-done.planes_ref = bf16[16,64,16,128]{3,2,1,0:T(8,128)(2,1)} async-done(((bf16[1,64,16,128]{3,2,1,0:T(8,128)(2,1)}), bf16[16,64,16,128]{3,2,1,0:T(8,128)(2,1)}) %all-gather.10.cloned.1.call-update) | async-done | bytes 4194320 | tf_op jit(solution)/shard_map/all_gather | solution.py:289
  119.7 24.5 %forward.1 = (f32[128,128]{1,0:T(8,128)}, f32[128,128]{1,0:T(8,128)}, bf16[128,256]{1,0:T(8,128)(2,1)}, f32[128,8,128]{2,1,0:T(8,128)}) custom-call(s32[3,128]{1,0:T(4,128)} %corner_ref.5, s32[1]{0:T(128)} %bitcast.11.slab_ref, f32[1]{0:T(128)} %bitcast.12.chosen_ref, bf16[16,64,16,128]{3,2,1,0:T(8,128)(2,1)} %all-gather.10.cloned.1.call-done.planes_ref, ...), custom_call_target="tpu_custom_call" | custom-call | flops 2147483648 | bytes 12582912 | tf_op jit(solution)/shard_map/forward/pallas_call | solution.py:367
  144.2 1.3 fusion.49
  145.5 5.0 %sort.14 = (s32[2048]{0:T(1024)S(1)}, s32[2048]{0:T(1024)}) sort(s32[2048]{0:T(1024)S(1)} %add_select_fusion.8, s32[2048]{0:T(1024)S(1)} %iota.28), dimensions={0}, to_apply=%region_1.2 | sort | flops 22528 | bytes 32768 | tf_op jit(solution)/shard_map/sort | solution.py:394
  150.5 1.3 multiply_reduce_fusion
  151.9 2.0 fusion.15
  153.9 2.1 concatenate.50
  156.6 5.7 %fusion.10 = (s32[2048,256]{1,0:T(8,128)}, s32[2048,256]{1,0:T(8,128)}) fusion(s16[16,128,256]{2,1,0:T(8,128)(2,1)S(1)} %slice.52, s32[2048]{0:T(1024)S(1)} %bitcast.91, s32[2048]{0:T(1024)S(1)} %bitcast.93), kind=kLoop, calls=%fused_computation.24 | loop fusion | flops 25690112 | bytes 5259264 | tf_op jit(solution)/shard_map/jit(_where)/select_n | solution.py:389
  162.3 19.1 %all-gather.12.cloned.1.call-done = bf16[2048,256]{1,0:T(8,128)(2,1)} async-done(((bf16[128,256]{1,0:T(8,128)(2,1)}), bf16[2048,256]{1,0:T(8,128)(2,1)}) %all-gather.12.cloned.1.call-update) | async-done | bytes 1048592 | tf_op jit(solution)/shard_map/all_gather | solution.py:381
  181.3 2.7 convert_element_type.54.term_ref
  184.0 10.8 %spread.1 = f32[1024,128]{1,0:T(8,128)} custom-call(s32[2048]{0:T(1024)} %compare_select_fusion.1.ids_ref, s32[1]{0:T(128)} %bitcast.6.count_ref, s32[2048]{0:T(1024)} %bitcast.92, s32[2048,256]{1,0:T(8,128)} %get-tuple-element.34.y_ref, s32[2048,256]{1,0:T(8,128)} %get-tuple-element.33.key_ref, f32[2048,256]{1,0:T(8,128)} %convert_element_type.54.term_ref), custom_call_target="tpu_custom_call" | custom-call | tf_op jit(solution)/shard_map/spread/pallas_call | solution.py:398
  194.9 1.2 copy.53
  196.1 1.4 bitcast_subtract_fusion
  198.1 1.0 convolution_convert_fusion
  199.3 0.7 pad_maximum_fusion
  200.1 60.4 %all-gather.14.cloned.1.call-done = bf16[1056,16,128]{2,1,0:T(8,128)(2,1)} async-done(((bf16[66,16,128]{2,1,0:T(8,128)(2,1)}), bf16[1056,16,128]{2,1,0:T(8,128)(2,1)}) %all-gather.14.cloned.1.call-update) | async-done | bytes 4325392 | tf_op jit(solution)/shard_map/all_gather | solution.py:442
  260.5 0.8 convert_reduce_fusion
  261.3 0.7 fusion.50
  262.0 20.7 %bend.1 = f32[128,128]{1,0:T(8,128)} custom-call(s32[3,128]{1,0:T(4,128)} %corner_ref.5, bf16[16,66,16,128]{3,2,1,0:T(8,128)(2,1)} %bitcast.80, bf16[256,256]{1,0:T(8,128)(2,1)} %get-tuple-element.36.kh_ref, bf16[256,256]{1,0:T(8,128)(2,1)} %get-tuple-element.35.kl_ref, s32[128,256]{1,0:T(8,128)} %get-tuple-element.39.y_ref, ...), custom_call_target="tpu_custom_call" | custom-call | tf_op jit(solution)/shard_map/bend/pallas_call | solution.py:443
  283.3 2.4 subtract_multiply_fusion
  (56 shorter events, 3.6 us)
Async XLA Ops:
  7.2 0.8 copy-start
  7.2 5.5 %copy-start.6 = (f32[128,128]{1,0:T(8,128)S(1)}, f32[128,128]{1,0:T(8,128)}, u32[]{:S(2)}) copy-start(f32[128,128]{1,0:T(8,128)} %param.14) | copy-start | bytes 196612
  7.2 4.9 %copy-start.2 = (f32[8,128,128]{2,1,0:T(8,128)S(1)}, f32[8,128,128]{2,1,0:T(8,128)}, u32[]{:S(2)}) copy-start(f32[8,128,128]{2,1,0:T(8,128)} %param.12) | copy-start | bytes 1572868
  7.2 58.1 %all-gather.8.cloned.1.call-start = ((), (), s32[]{:S(2)}) async-start(), calls=%async_computation | async-start | bytes 4456448 | tf_op jit(solution)/shard_map/all_gather | solution.py:289
  9.6 4.7 %copy-start.1 = (f32[8,128,128]{2,1,0:T(8,128)S(1)}, f32[8,128,128]{2,1,0:T(8,128)}, u32[]{:S(2)}) copy-start(f32[8,128,128]{2,1,0:T(8,128)} %param.11) | copy-start | bytes 1572868
  12.0 107.7 %all-gather.10.cloned.1.call-start = ((), (), s32[]{:S(2)}) async-start(), calls=%async_computation.1 | async-start | bytes 4456448 | tf_op jit(solution)/shard_map/all_gather | solution.py:289
  12.7 2.9 copy-start.10
  12.7 2.9 copy-start.9
  13.3 3.4 %copy-start.5 = (s32[128,128]{1,0:T(8,128)S(1)}, s32[128,128]{1,0:T(8,128)}, u32[]{:S(2)}) copy-start(s32[128,128]{1,0:T(8,128)} %labels_ref.1) | copy-start | bytes 196612
  14.2 2.5 copy-start.11
  14.2 3.1 %copy-start.7 = (s32[128,256]{1,0:T(8,128)S(1)}, s32[128,256]{1,0:T(8,128)}, u32[]{:S(2)}) copy-start(s32[128,256]{1,0:T(8,128)} %param.18) | copy-start | bytes 393220
  14.2 167.1 %all-gather.12.cloned.1.call-start = ((), (), s32[]{:S(2)}) async-start(), calls=%async_computation.2 | async-start | bytes 1114112 | tf_op jit(solution)/shard_map/all_gather | solution.py:381
  119.7 30.9 %copy-start.8 = (f32[128,128]{1,0:T(8,128)S(1)}, f32[128,128]{1,0:T(8,128)}, u32[]{:S(2)}) copy-start(f32[128,128]{1,0:T(8,128)} %get-tuple-element.18.latent_ref) | copy-start | bytes 196612
  119.7 30.9 %copy-start.12 = (f32[5]{0:T(128)S(1)}, f32[5]{0:T(128)}, u32[]{:S(2)}) copy-start(f32[5]{0:T(128)} %param.20) | copy-start | bytes 64
  119.7 32.2 %copy-start.3 = (f32[8,128,128]{1,0,2:T(8,128)S(1)}, f32[8,128,128]{1,0,2:T(8,128)}, u32[]{:S(2)}) copy-start(f32[8,128,128]{1,0,2:T(8,128)} %copy.57) | copy-start | bytes 1572868
  144.2 116.3 %all-gather.14.cloned.1.call-start = ((), (), s32[]{:S(2)}) async-start(), calls=%async_computation.3 | async-start | bytes 4595712 | tf_op jit(solution)/shard_map/all_gather | solution.py:442
  197.5 85.2 %copy-start.4 = (f32[8,128,128]{2,1,0:T(8,128)}, f32[8,128,128]{2,1,0:T(8,128)S(1)}, u32[]{:S(2)}) copy-start(f32[8,128,128]{2,1,0:T(8,128)S(1)} %get-tuple-element.29) | copy-start | bytes 1572868
Sparse Core Ops, SparseCore 0:
  12.2 53.0 all-gather.7
  68.0 51.6 all-gather.9
  144.3 36.9 all-gather.11
  200.2 60.2 all-gather.13
